TPU v7x, 32 devices: a whole 2x2x4 slice. The times are simulated.
32 devices in a mesh: gene: 8 (over z, x), cell: 4 (over y, core).
Axes of the slice: x: 2, y: 2, z: 4, core: 2. Of those that a mesh axis runs over, the one named last changes fastest.
Arguments:
- gene_tokens: bfloat16 [16, 4096, 768], P('cell', 'gene')
- latents: bfloat16 [64, 768], replicated, may hold values from -6 to 6
- head_temp: float32 [12], replicated, may hold values from 1.5 to 4
- w_key: bfloat16 [768, 768], replicated, may hold values from -0.21875 to 0.21875
- w_value: bfloat16 [768, 768], replicated, may hold values from -0.21875 to 0.21875
- w_out: bfloat16 [768, 768], replicated, may hold values from -0.21875 to 0.21875
- w_set_qkv: bfloat16 [768, 2304], replicated, may hold values from -0.21875 to 0.21875
- w_set_out: bfloat16 [768, 768], replicated, may hold values from -0.21875 to 0.21875
- set_ids: int32 [16], P('cell'), may hold values from 0 to 7, as said below
Outputs:
- latent_states: bfloat16 [16, 64, 768], P('cell', 'gene')
- set_states: bfloat16 [16, 768], P('cell')
Inputs may be any that keep to these rules, and one draw needn't show every extreme that they name: `set_ids`: set s is held by index s mod 4 of cell. At most 2 cells of one device's block belong to sets held by one index, and in every draw one index holds the sets of exactly 2 cells of every device's block.
All inputs are finite; a program needn't handle non-finite values.
Results may differ from a plain program's by a relative error of at most 0.012.
Values may be sent and summed in bfloat16 or wider, within the bound.
A program may use at most 64 MiB of HBM per device.

v0:
```python
import math
import jax
import jax.numpy as jnp
from jax import lax
from jax.sharding import PartitionSpec as P

EPSILON = 1e-06


def head_norm(array, head_count):
    shaped = array.reshape(array.shape[:-1] + (head_count, array.shape[-1] // head_count))
    return shaped * lax.rsqrt(jnp.mean(shaped * shaped, axis=-1, keepdims=True) + EPSILON)


def set_project(inputs, w_set_qkv, head_count):
    model_width = inputs.shape[1]
    head_size = model_width // head_count
    projected = jnp.dot(inputs, w_set_qkv, preferred_element_type=jnp.float32)
    queries = (head_norm(projected[:, :model_width], head_count) / math.sqrt(head_size)).astype(
        jnp.bfloat16
    )
    key_rows = head_norm(projected[:, model_width : 2 * model_width], head_count).astype(
        jnp.bfloat16
    )
    value_rows = (
        projected[:, 2 * model_width :]
        .reshape(inputs.shape[0], head_count, head_size)
        .astype(jnp.bfloat16)
    )
    return (queries, key_rows, value_rows)


def set_attend(queries, key_rows, value_rows, query_ids, key_ids, residual, w_set_out):
    scores = jnp.einsum("qhe,khe->hqk", queries, key_rows, preferred_element_type=jnp.float32)
    matching = query_ids[:, None] == key_ids[None, :]
    weights = jnp.where(matching[None], jnp.exp(scores), 0.0)
    totals = jnp.sum(weights, axis=2)
    numerator = jnp.einsum(
        "hqk,khe->qhe", weights.astype(jnp.bfloat16), value_rows, preferred_element_type=jnp.float32
    )
    attended = (
        (numerator / jnp.transpose(totals)[:, :, None])
        .reshape(queries.shape[0], -1)
        .astype(jnp.bfloat16)
    )
    return (
        residual.astype(jnp.float32)
        + jnp.dot(attended, w_set_out, preferred_element_type=jnp.float32)
    ).astype(jnp.bfloat16)


def on_device(
    gene_tokens, latents, head_temp, w_key, w_value, w_out, w_set_qkv, w_set_out, set_ids
):
    cell_count, gene_count, model_width = gene_tokens.shape
    latent_count = latents.shape[0]
    head_count = head_temp.shape[0]
    head_size = model_width // head_count
    queries = (
        head_norm(latents.astype(jnp.float32), head_count)
        * (head_temp[:, None] / math.sqrt(head_size))
    ).astype(jnp.bfloat16)
    key_rows = head_norm(
        jnp.einsum("cgd,de->cge", gene_tokens, w_key, preferred_element_type=jnp.float32),
        head_count,
    ).astype(jnp.bfloat16)
    value_rows = jnp.einsum(
        "cgd,de->cge", gene_tokens, w_value, preferred_element_type=jnp.float32
    ).astype(jnp.bfloat16)
    value_rows = value_rows.reshape(cell_count, gene_count, head_count, head_size)
    scores = jnp.einsum("lhe,cghe->chlg", queries, key_rows, preferred_element_type=jnp.float32)
    weights = jnp.exp(scores)
    totals = jnp.transpose(jnp.sum(weights, axis=3), (0, 2, 1))
    numerator = jnp.einsum(
        "chlg,cghe->clhe",
        weights.astype(jnp.bfloat16),
        value_rows,
        preferred_element_type=jnp.float32,
    )
    numerator = numerator.reshape(cell_count, latent_count, model_width)
    numerator, totals = (
        lax.psum(numerator.astype(jnp.bfloat16), "gene").astype(jnp.float32),
        lax.psum(totals.astype(jnp.bfloat16), "gene").astype(jnp.float32),
    )
    portion = latent_count // lax.axis_size("gene")
    first_row = lax.axis_index("gene") * portion
    attended = (
        numerator.reshape(cell_count, latent_count, head_count, head_size) / totals[..., None]
    )
    attended = attended.reshape(cell_count, latent_count, model_width).astype(jnp.bfloat16)
    mixed_rows = latents.astype(jnp.float32)[None] + jnp.einsum(
        "cld,de->cle", attended, w_out, preferred_element_type=jnp.float32
    )
    pooled = jnp.mean(mixed_rows, axis=1)
    latent_states = lax.dynamic_slice_in_dim(mixed_rows, first_row, portion, 1).astype(jnp.bfloat16)
    set_input = (
        pooled * lax.rsqrt(jnp.mean(pooled * pooled, axis=1, keepdims=True) + EPSILON)
    ).astype(jnp.bfloat16)
    every_input, every_ids = (
        lax.all_gather(set_input, "cell", axis=0, tiled=True),
        lax.all_gather(set_ids, "cell", axis=0, tiled=True),
    )
    set_queries, set_keys, set_values = set_project(every_input, w_set_qkv, head_count)
    own_queries = lax.dynamic_slice_in_dim(
        set_queries, lax.axis_index("cell") * cell_count, cell_count, 0
    )
    set_states = set_attend(
        own_queries, set_keys, set_values, set_ids, every_ids, set_input, w_set_out
    )
    return (latent_states, set_states)


def solution(mesh):
    in_specs = (P("cell", "gene", None), P(), P(), P(), P(), P(), P(), P(), P("cell"))
    out_specs = (P("cell", "gene", None), P("cell", None))
    return jax.shard_map(
        on_device, mesh=mesh, in_specs=in_specs, out_specs=out_specs, check_vma=False
    )
```

profile of v0, /device:TPU:0, one launch (start us, length us, event | category | flops | bytes accessed | tf_op | source)
XLA Modules:
  0.0 154.6 jit_solution(15478738839907730430)
XLA Ops:
  7.2 2.0 %reshape.103 = f32[64,12,64]{2,1,0:T(8,128)} reshape(bf16[64,768]{1,0:T(8,128)(2,1)} %param.10) | data formatting | bytes 294912 | tf_op jit(solution)/shard_map/reshape | solution.py:11
  9.2 1.3 multiply_reduce_fusion.1
  10.5 0.6 add_rsqrt_fusion.1
  11.1 0.7 broadcast_multiply_fusion
  11.8 5.0 %fusion.8 = f32[4,512,768]{1,2,0:T(8,128)S(1)} fusion(bf16[4,512,768]{2,1,0:T(8,128)(2,1)} %param.9, bf16[768,768]{1,0:T(8,128)(2,1)} %param.12), kind=kOutput, calls=%fused_computation.12 | convolution fusion | flops 2415919104 | bytes 10616832 | tf_op jit(solution)/shard_map/cgd,de->cge/dot_general | solution.py:64
  16.8 1.0 multiply_reduce_fusion
  17.8 2.2 %copy-done.1 = f32[4,512,768]{1,2,0:T(8,128)} copy-done((f32[4,512,768]{1,2,0:T(8,128)}, f32[4,512,768]{1,2,0:T(8,128)S(1)}, u32[]{:S(2)}) %copy-start.1) | copy-done | bytes 6291480
  20.0 0.7 add_rsqrt_fusion
  20.7 0.3 copy-done.3
  21.0 0.4 copy-done.4
  21.4 4.0 %convolution_convert_fusion = bf16[4,512,768]{2,1,0:T(8,128)(2,1)} fusion(bf16[4,512,768]{2,1,0:T(8,128)(2,1)S(1)} %copy-done.3, bf16[768,768]{1,0:T(8,128)(2,1)S(1)} %copy-done.4), kind=kOutput, calls=%fused_computation.8 | convolution fusion | flops 2417491968 | bytes 7471104 | tf_op jit(solution)/shard_map/cgd,de->cge/dot_general | solution.py:67
  25.3 4.7 %copy.30 = bf16[4,512,768]{1,2,0:T(8,128)(2,1)} copy(bf16[4,512,768]{2,1,0:T(8,128)(2,1)} %convolution_convert_fusion) | data formatting | bytes 6291456 | tf_op jit(solution)/shard_map/convert_element_type | solution.py:69
  30.1 1.2 fusion.15
  31.4 4.8 %bitcast_reduce_fusion = (bf16[4,12,64]{2,0,1:T(4,128)(2,1)}, f32[12,4,512,64]{2,3,1,0:T(8,128)S(1)}) fusion(bf16[64,12,64,1]{2,1,0,3:T(8,128)(2,1)S(1)} %fusion.15, f32[4,512,12,64]{1,3,2,0:T(8,128)} %bitcast.45, f32[4,512,12]{1,2,0:T(8,128)} %add_rsqrt_fusion), kind=kOutput, calls=%fused_computation | convolution fusion | flops 206042112 | bytes 12785664 | tf_op jit(solution)/shard_map/lhe,cghe->chlg/dot_general | solution.py:71
  36.1 1.9 %fusion.4 = bf16[4,12,64,64]{3,2,1,0:T(8,128)(2,1)} fusion(bf16[4,512,12,64]{1,3,2,0:T(8,128)(2,1)S(1)} %bitcast.46, f32[12,4,512,64]{2,3,1,0:T(8,128)S(1)} %get-tuple-element.5), kind=kOutput, calls=%fused_computation.9 | convolution fusion | flops 203096064 | bytes 9830400 | tf_op jit(solution)/shard_map/chlg,cghe->clhe/dot_general | solution.py:74
  38.0 2.1 %copy.35 = bf16[4,64,768]{2,1,0:T(8,128)(2,1)} copy(bf16[4,64,768]{1,2,0:T(8,128)(2,1)} %bitcast.47) | data formatting | bytes 786432 | tf_op jit(solution)/shard_map/convert_element_type | solution.py:82
  40.2 1.6 %convert_element_type.71 = f32[64,768]{1,0:T(8,128)} convert(bf16[64,768]{1,0:T(8,128)(2,1)} %param.10) | non-fusion elementwise | flops 49152 | bytes 294912 | tf_op jit(solution)/shard_map/convert_element_type | solution.py:91
  41.8 38.9 %psum.15 = bf16[4,64,12]{1,0,2:T(4,128)(2,1)S(1)} all-reduce(bf16[4,64,12]{1,0,2:T(4,128)(2,1)} %bitcast.48), channel_id=1, replica_groups=mesh['gene'=8,'cell'=4] {'gene'}, use_global_device_ids=true, to_apply=%region_4.0 | all-reduce | flops 3072 | bytes 12288 | tf_op jit(solution)/shard_map/psum | solution.py:83
  80.7 0.8 copy.36
  81.5 2.9 %div.60 = f32[4,64,12,64]{3,2,1,0:T(8,128)} broadcast(f32[4,64,12]{2,1,0:T(8,128)} %copy.36), dimensions={0,1,2} | broadcast | bytes 798720 | tf_op jit(solution)/shard_map/div | solution.py:88
  84.4 2.7 %div.61 = f32[4,64,768]{2,1,0:T(8,128)} reshape(f32[4,64,12,64]{3,2,1,0:T(8,128)} %div.60) | data formatting | bytes 1572864 | tf_op jit(solution)/shard_map/div | solution.py:88
  87.1 1.2 dynamic-slice
  89.0 0.2 dynamic-update-slice
  89.2 4.9 %all-reduce = s32[16]{0:T(128)S(1)} all-reduce(s32[16]{0:T(128)S(1)} %dynamic-update-slice), channel_id=1, replica_groups=mesh['gene'=8,'cell'=4] {'cell'}, use_global_device_ids=true, to_apply=%add | all-reduce | flops 16 | bytes 128
  94.2 0.6 broadcast_compare_fusion
  94.8 19.7 %all-reduce.3.cloned.1.call-done = bf16[4,64,768]{2,1,0:T(8,128)(2,1)} async-done(((bf16[4,64,768]{2,1,0:T(8,128)(2,1)}), bf16[4,64,768]{2,1,0:T(8,128)(2,1)}) %all-reduce.3.cloned.1.call-update) | async-done | bytes 393232 | tf_op jit(solution)/shard_map/psum | solution.py:82
  114.5 2.9 %fusion.28 = (f32[4,768]{1,0:T(4,128)S(1)}, bf16[4,64,768]{2,1,0:T(8,128)(2,1)}) fusion(bf16[768,768]{1,0:T(8,128)(2,1)} %param.14, f32[4,64,768]{2,1,0:T(8,128)} %div.61, bf16[4,64,768]{2,1,0:T(8,128)(2,1)} %all-reduce.3.cloned.1.call-done, f32[64,768]{1,0:T(8,128)} %convert_element_type.71), kind=kOutput, calls=%fused_computation.55 | convolution fusion | flops 303166464 | bytes 2961408 | tf_op jit(solution)/shard_map/cld,de->cle/dot_general | solution.py:91
  117.5 5.6 %all-gather = bf16[4,4,768]{2,1,0:T(4,128)(2,1)} all-gather(bf16[1,4,768]{2,1,0:T(4,128)(2,1)S(1)} %fusion.26), channel_id=1, replica_groups=mesh['gene'=8,'cell'=4] {'cell'}, dimensions={0}, use_global_device_ids=true | all-gather | bytes 30720 | tf_op jit(solution)/shard_map/all_gather | solution.py:100
  123.2 1.4 reshape.110
  124.5 1.3 fusion.30
  125.9 0.7 fusion.27
  126.5 0.6 slice.17
  127.1 1.5 reshape.105
  128.6 1.0 multiply_reduce_fusion.2
  129.7 1.6 %multiply_convert_fusion.2 = bf16[16,12,64]{2,1,0:T(8,128)(2,1)} fusion(f32[16,12,64]{2,1,0:T(8,128)} %reshape.105, f32[16,12]{1,0:T(8,128)S(1)} %add_rsqrt_fusion.2), kind=kLoop, calls=%fused_computation.27 | loop fusion | flops 24576 | bytes 74496 | tf_op jit(solution)/shard_map/convert_element_type | solution.py:22
  131.3 1.5 reshape.104
  132.8 1.0 multiply_reduce_fusion.3
  133.8 1.4 constant_dynamic-slice_fusion
  135.2 0.6 add_rsqrt_fusion.3
  135.8 1.4 copy.37
  137.2 1.4 constant_dynamic-slice_fusion.1
  138.6 1.5 convert_element_type.87
  140.0 1.2 fusion.29
  141.2 1.0 fusion.13
  142.2 0.6 copy.41
  142.8 1.4 convert_element_type.92
  144.2 2.2 %fusion.14 = bf16[4,768]{1,0:T(4,128)(2,1)} fusion(bf16[4,768]{1,0:T(4,128)(2,1)} %convert_element_type.92, bf16[768,768]{1,0:T(8,128)(2,1)} %param.16, f32[4,768]{1,0:T(4,128)S(1)} %get-tuple-element.6, f32[4]{0:T(128)S(1)} %rsqrt_multiply_fusion), kind=kOutput, calls=%fused_computation.21 | convolution fusion | flops 4733952 | bytes 1204240 | tf_op jit(solution)/shard_map/dot_general | solution.py:48
  146.3 1.4 dynamic-slice_convert_fusion
  (16 shorter events, 0.3 us)
Async XLA Ops:
  7.2 117.4 %copy-start = (bf16[768,2304]{1,0:T(8,128)(2,1)S(1)}, bf16[768,2304]{1,0:T(8,128)(2,1)}, u32[]{:S(2)}) copy-start(bf16[768,2304]{1,0:T(8,128)(2,1)} %param.15) | copy-start | bytes 10616836
  7.2 107.3 %all-reduce.3.cloned.1.call-start = ((), (), s32[]{:S(2)}) async-start(), calls=%async_computation | async-start | bytes 786432 | tf_op jit(solution)/shard_map/psum | solution.py:82
  16.8 3.2 %copy-start.1 = (f32[4,512,768]{1,2,0:T(8,128)}, f32[4,512,768]{1,2,0:T(8,128)S(1)}, u32[]{:S(2)}) copy-start(f32[4,512,768]{1,2,0:T(8,128)S(1)} %fusion.8) | copy-start | bytes 18874372
  16.8 4.2 %copy-start.3 = (bf16[4,512,768]{2,1,0:T(8,128)(2,1)S(1)}, bf16[4,512,768]{2,1,0:T(8,128)(2,1)}, u32[]{:S(2)}) copy-start(bf16[4,512,768]{2,1,0:T(8,128)(2,1)} %param.9) | copy-start | bytes 9437188
  16.8 4.5 %copy-start.4 = (bf16[768,768]{1,0:T(8,128)(2,1)S(1)}, bf16[768,768]{1,0:T(8,128)(2,1)}, u32[]{:S(2)}) copy-start(bf16[768,768]{1,0:T(8,128)(2,1)} %param.13) | copy-start | bytes 3538948
  31.3 4.8 %copy-start.2 = (bf16[4,512,768]{1,2,0:T(8,128)(2,1)S(1)}, bf16[4,512,768]{1,2,0:T(8,128)(2,1)}, u32[]{:S(2)}) copy-start(bf16[4,512,768]{1,2,0:T(8,128)(2,1)} %copy.30) | copy-start | bytes 9437188
  40.2 48.8 %copy-start.5 = (s32[4]{0:T(128)S(1)}, s32[4]{0:T(128)}, u32[]{:S(2)}) copy-start(s32[4]{0:T(128)} %param.17) | copy-start | bytes 52
Sparse Core Ops, SparseCore 0:
  40.3 74.0 all-reduce.2
where the time goes:
time: 156 us; the launch traced here: 155 us
  blocking collectives  49.5 us (32%)
  local copies, waits for them, and re-layouts  34.3 us (22%)
  matrix products  24.2 us (16%)
  waiting for transfers between devices  19.7 us (13%)
  between operations  14.8 us (9%)
  other arithmetic  12.1 us (8%)
    psum x1, blocking collectives, on_device(): lax.psum(totals.astype(jnp.bfloat16), 'gene').astype(jnp.float32)  38.9 us
    psum x1, waiting for transfers between devices, on_device(): lax.psum(numerator.astype(jnp.bfloat16), 'gene').astype(jnp.float32)  19.7 us
    unnamed x16, local copies, waits for them, and re-layouts  5.73 us
    all_gather x1, blocking collectives, on_device(): lax.all_gather(set_input, 'cell', axis=0, tiled=True)  5.63 us
    div x2, local copies, waits for them, and re-layouts, on_device(): numerator.reshape(cell_count, latent_count, head_count, head_size)  5.58 us
    reshape x3, local copies, waits for them, and re-layouts, head_norm(): array.reshape(array.shape[:-1] + (head_count, array.shape[-1] // head_cou...  5.07 us
    dot_general x1, matrix products, on_device(): jnp.einsum('cgd,de->cge', gene_tokens, w_key, preferred_element_type=jnp....  5.02 us
    unnamed x1, blocking collectives  4.93 us
  transfers between devices with their start and end apart: 1, of which 1 were waited for; matrix products, arithmetic and copies ran while one was open for 6% of the time, Pallas kernels for 0%

commit v1 on v0

--- a/solution.py
+++ b/solution.py
@@ -5,6 +5,11 @@
 from jax.sharding import PartitionSpec as P
 
 EPSILON = 1e-06
+
+
+def add_all(x, axis):
+    parts = lax.all_gather(x, axis)
+    return jnp.sum(parts, axis=0)
 
 
 def head_norm(array, head_count):
@@ -79,7 +84,7 @@
     )
     numerator = numerator.reshape(cell_count, latent_count, model_width)
     numerator, totals = (
-        lax.psum(numerator.astype(jnp.bfloat16), "gene").astype(jnp.float32),
+        add_all(numerator.astype(jnp.bfloat16), "gene").astype(jnp.float32),
         lax.psum(totals.astype(jnp.bfloat16), "gene").astype(jnp.float32),
     )
     portion = latent_count // lax.axis_size("gene")

time: 156 us -> 148 us (0.949)
  waiting for transfers between devices: 19.7 us -> 8.68 us
  other arithmetic: 12.1 us -> 15.2 us
    psum x1 -> x0, waiting for transfers between devices: 19.7 us -> none  [on_device(): lax.psum(numerator.astype(jnp.bfloat16), 'gene').astype(jnp.float32)]
    all_gather x0 -> x1, waiting for transfers between devices: none -> 8.66 us  [add_all(): parts = lax.all_gather(x, axis)]
    reduce_sum x0 -> x1, other arithmetic: none -> 3.17 us  [add_all(): return jnp.sum(parts, axis=0)]
  transfers between devices with their start and end apart: 1 -> 1, of which waited for: 1 -> 1; matrix products, arithmetic and copies ran while one was open for 6% -> 7% of each run, Pallas kernels for 0% -> 0%
where the time goes in v1:
time: 148 us; the launch traced here: 147 us
  blocking collectives  49.8 us (34%)
  local copies, waits for them, and re-layouts  34.3 us (23%)
  matrix products  24.2 us (16%)
  other arithmetic  15.2 us (10%)
  between operations  14.8 us (10%)
  waiting for transfers between devices  8.68 us (6%)
    psum x1, blocking collectives, on_device(): lax.psum(totals.astype(jnp.bfloat16), 'gene').astype(jnp.float32)  39.3 us
    all_gather x1, waiting for transfers between devices, add_all(): parts = lax.all_gather(x, axis)  8.66 us
    unnamed x16, local copies, waits for them, and re-layouts  5.73 us
    all_gather x1, blocking collectives, on_device(): lax.all_gather(set_input, 'cell', axis=0, tiled=True)  5.63 us
    div x2, local copies, waits for them, and re-layouts, on_device(): numerator.reshape(cell_count, latent_count, head_count, head_size)  5.6 us
    reshape x3, local copies, waits for them, and re-layouts, head_norm(): array.reshape(array.shape[:-1] + (head_count, array.shape[-1] // head_cou...  5.07 us
    dot_general x1, matrix products, on_device(): jnp.einsum('cgd,de->cge', gene_tokens, w_key, preferred_element_type=jnp....  5.02 us
    unnamed x1, blocking collectives  4.85 us
  transfers between devices with their start and end apart: 1, of which 1 were waited for; matrix products, arithmetic and copies ran while one was open for 7% of the time, Pallas kernels for 0%

profile of v1, /device:TPU:0, one launch (start us, length us, event | category | flops | bytes accessed | tf_op | source)
XLA Modules:
  0.0 147.0 jit_solution(15994579717606464118)
XLA Ops:
  7.2 2.0 %reshape.114 = f32[64,12,64]{2,1,0:T(8,128)} reshape(bf16[64,768]{1,0:T(8,128)(2,1)} %param.10) | data formatting | bytes 294912 | tf_op jit(solution)/shard_map/reshape | solution.py:16
  9.2 1.3 multiply_reduce_fusion.1
  10.5 0.6 add_rsqrt_fusion.1
  11.1 0.7 broadcast_multiply_fusion
  11.8 5.0 %fusion.8 = f32[4,512,768]{1,2,0:T(8,128)S(1)} fusion(bf16[4,512,768]{2,1,0:T(8,128)(2,1)} %param.9, bf16[768,768]{1,0:T(8,128)(2,1)} %param.12), kind=kOutput, calls=%fused_computation.12 | convolution fusion | flops 2415919104 | bytes 10616832 | tf_op jit(solution)/shard_map/cgd,de->cge/dot_general | solution.py:69
  16.8 1.0 multiply_reduce_fusion
  17.8 2.2 %copy-done.1 = f32[4,512,768]{1,2,0:T(8,128)} copy-done((f32[4,512,768]{1,2,0:T(8,128)}, f32[4,512,768]{1,2,0:T(8,128)S(1)}, u32[]{:S(2)}) %copy-start.1) | copy-done | bytes 6291480
  20.0 0.7 add_rsqrt_fusion
  20.7 0.3 copy-done.3
  21.0 0.4 copy-done.4
  21.4 4.0 %convolution_convert_fusion = bf16[4,512,768]{2,1,0:T(8,128)(2,1)} fusion(bf16[4,512,768]{2,1,0:T(8,128)(2,1)S(1)} %copy-done.3, bf16[768,768]{1,0:T(8,128)(2,1)S(1)} %copy-done.4), kind=kOutput, calls=%fused_computation.8 | convolution fusion | flops 2417491968 | bytes 7471104 | tf_op jit(solution)/shard_map/cgd,de->cge/dot_general | solution.py:72
  25.3 4.7 %copy.43 = bf16[4,512,768]{1,2,0:T(8,128)(2,1)} copy(bf16[4,512,768]{2,1,0:T(8,128)(2,1)} %convolution_convert_fusion) | data formatting | bytes 6291456 | tf_op jit(solution)/shard_map/convert_element_type | solution.py:74
  30.1 1.2 fusion.15
  31.4 4.8 %bitcast_reduce_fusion = (bf16[4,12,64]{2,0,1:T(4,128)(2,1)}, f32[12,4,512,64]{2,3,1,0:T(8,128)S(1)}) fusion(bf16[64,12,64,1]{2,1,0,3:T(8,128)(2,1)S(1)} %fusion.15, f32[4,512,12,64]{1,3,2,0:T(8,128)} %bitcast.45, f32[4,512,12]{1,2,0:T(8,128)} %add_rsqrt_fusion), kind=kOutput, calls=%fused_computation | convolution fusion | flops 206042112 | bytes 12785664 | tf_op jit(solution)/shard_map/lhe,cghe->chlg/dot_general | solution.py:76
  36.1 1.9 %fusion.4 = bf16[4,12,64,64]{3,2,1,0:T(8,128)(2,1)} fusion(bf16[4,512,12,64]{1,3,2,0:T(8,128)(2,1)S(1)} %bitcast.46, f32[12,4,512,64]{2,3,1,0:T(8,128)S(1)} %get-tuple-element.5), kind=kOutput, calls=%fused_computation.9 | convolution fusion | flops 203096064 | bytes 9830400 | tf_op jit(solution)/shard_map/chlg,cghe->clhe/dot_general | solution.py:79
  38.0 2.1 %copy.48 = bf16[1,4,64,768]{3,2,1,0:T(8,128)(2,1)} copy(bf16[1,4,64,768]{2,3,1,0:T(8,128)(2,1)} %bitcast.47) | data formatting | bytes 786432 | tf_op jit(solution)/shard_map/convert_element_type | solution.py:87
  40.2 1.6 %convert_element_type.82 = f32[64,768]{1,0:T(8,128)} convert(bf16[64,768]{1,0:T(8,128)(2,1)} %param.10) | non-fusion elementwise | flops 49152 | bytes 294912 | tf_op jit(solution)/shard_map/convert_element_type | solution.py:96
  41.8 39.3 %psum.7 = bf16[4,64,12]{1,0,2:T(4,128)(2,1)S(1)} all-reduce(bf16[4,64,12]{1,0,2:T(4,128)(2,1)} %bitcast.48), channel_id=1, replica_groups=mesh['gene'=8,'cell'=4] {'gene'}, use_global_device_ids=true, to_apply=%region_4.0 | all-reduce | flops 3072 | bytes 12288 | tf_op jit(solution)/shard_map/psum | solution.py:88
  81.1 0.8 copy.51
  81.8 2.9 %div.60 = f32[4,64,12,64]{3,2,1,0:T(8,128)} broadcast(f32[4,64,12]{2,1,0:T(8,128)} %copy.51), dimensions={0,1,2} | broadcast | bytes 798720 | tf_op jit(solution)/shard_map/div | solution.py:93
  84.7 2.7 %div.61 = f32[4,64,768]{2,1,0:T(8,128)} reshape(f32[4,64,12,64]{3,2,1,0:T(8,128)} %div.60) | data formatting | bytes 1572864 | tf_op jit(solution)/shard_map/div | solution.py:93
  87.5 1.2 dynamic-slice
  89.6 4.9 %all-reduce = s32[16]{0:T(128)S(1)} all-reduce(s32[16]{0:T(128)S(1)} %dynamic-update-slice), channel_id=1, replica_groups=mesh['gene'=8,'cell'=4] {'cell'}, use_global_device_ids=true, to_apply=%add | all-reduce | flops 16 | bytes 128
  94.5 0.6 broadcast_compare_fusion
  95.0 8.7 %all-gather.3.cloned.1.call-done = bf16[8,4,64,768]{3,2,1,0:T(8,128)(2,1)} async-done(((bf16[1,4,64,768]{3,2,1,0:T(8,128)(2,1)}), bf16[8,4,64,768]{3,2,1,0:T(8,128)(2,1)}) %all-gather.3.cloned.1.call-update) | async-done | bytes 3145744 | tf_op jit(solution)/shard_map/all_gather | solution.py:11
  103.7 3.2 %reduce_sum.86 = bf16[4,64,768]{2,1,0:T(8,128)(2,1)} reduce(bf16[8,4,64,768]{3,2,1,0:T(8,128)(2,1)} %all-gather.3.cloned.1.call-done, bf16[]{:T(256)} %constant.18.clone.1), dimensions={0}, to_apply=%region_2.0 | reduce | flops 1376256 | bytes 3538946 | tf_op jit(solution)/shard_map/reduce_sum | solution.py:12
  106.9 2.9 %fusion.28 = (f32[4,768]{1,0:T(4,128)S(1)}, bf16[4,64,768]{2,1,0:T(8,128)(2,1)}) fusion(bf16[768,768]{1,0:T(8,128)(2,1)} %param.14, f32[4,64,768]{2,1,0:T(8,128)} %div.61, bf16[4,64,768]{2,1,0:T(8,128)(2,1)} %reduce_sum.86, f32[64,768]{1,0:T(8,128)} %convert_element_type.82), kind=kOutput, calls=%fused_computation.55 | convolution fusion | flops 303166464 | bytes 2961408 | tf_op jit(solution)/shard_map/cld,de->cle/dot_general | solution.py:96
  110.0 5.6 %all-gather = bf16[4,4,768]{2,1,0:T(4,128)(2,1)} all-gather(bf16[1,4,768]{2,1,0:T(4,128)(2,1)S(1)} %fusion.26), channel_id=1, replica_groups=mesh['gene'=8,'cell'=4] {'cell'}, dimensions={0}, use_global_device_ids=true | all-gather | bytes 30720 | tf_op jit(solution)/shard_map/all_gather | solution.py:105
  115.6 1.4 reshape.121
  117.0 1.3 fusion.30
  118.3 0.7 fusion.27
  118.9 0.6 slice.17
  119.5 1.5 %reshape.116 = f32[16,12,64]{2,1,0:T(8,128)} reshape(f32[16,768]{1,0:T(8,128)} %get-tuple-element.3) | data formatting | bytes 98304 | tf_op jit(solution)/shard_map/reshape | solution.py:16
  121.1 1.0 multiply_reduce_fusion.2
  122.1 1.6 %multiply_convert_fusion.2 = bf16[16,12,64]{2,1,0:T(8,128)(2,1)} fusion(f32[16,12,64]{2,1,0:T(8,128)} %reshape.116, f32[16,12]{1,0:T(8,128)S(1)} %add_rsqrt_fusion.2), kind=kLoop, calls=%fused_computation.27 | loop fusion | flops 24576 | bytes 74496 | tf_op jit(solution)/shard_map/convert_element_type | solution.py:27
  123.7 1.5 %reshape.115 = f32[16,12,64]{2,1,0:T(8,128)} reshape(f32[16,768]{1,0:T(8,128)} %get-tuple-element.2) | data formatting | bytes 98304 | tf_op jit(solution)/shard_map/reshape | solution.py:16
  125.2 1.0 multiply_reduce_fusion.3
  126.3 1.4 constant_dynamic-slice_fusion
  127.6 0.6 add_rsqrt_fusion.3
  128.2 1.4 copy.52
  129.6 1.4 constant_dynamic-slice_fusion.1
  131.0 1.5 convert_element_type.98
  132.4 1.2 fusion.29
  133.6 1.0 fusion.13
  134.6 0.6 copy.56
  135.2 1.4 convert_element_type.103
  136.6 2.2 %fusion.14 = bf16[4,768]{1,0:T(4,128)(2,1)} fusion(bf16[4,768]{1,0:T(4,128)(2,1)} %convert_element_type.103, bf16[768,768]{1,0:T(8,128)(2,1)} %param.16, f32[4,768]{1,0:T(4,128)S(1)} %get-tuple-element.6, f32[4]{0:T(128)S(1)} %rsqrt_multiply_fusion), kind=kOutput, calls=%fused_computation.21 | convolution fusion | flops 4733952 | bytes 1204240 | tf_op jit(solution)/shard_map/dot_general | solution.py:53
  138.7 1.4 dynamic-slice_convert_fusion
  (17 shorter events, 0.5 us)
Async XLA Ops:
  7.2 109.8 %copy-start = (bf16[768,2304]{1,0:T(8,128)(2,1)S(1)}, bf16[768,2304]{1,0:T(8,128)(2,1)}, u32[]{:S(2)}) copy-start(bf16[768,2304]{1,0:T(8,128)(2,1)} %param.15) | copy-start | bytes 10616836
  7.2 96.5 %all-gather.3.cloned.1.call-start = ((), (), s32[]{:S(2)}) async-start(), calls=%async_computation | async-start | bytes 3538944 | tf_op jit(solution)/shard_map/all_gather | solution.py:11
  16.8 3.2 %copy-start.1 = (f32[4,512,768]{1,2,0:T(8,128)}, f32[4,512,768]{1,2,0:T(8,128)S(1)}, u32[]{:S(2)}) copy-start(f32[4,512,768]{1,2,0:T(8,128)S(1)} %fusion.8) | copy-start | bytes 18874372
  16.8 4.2 %copy-start.3 = (bf16[4,512,768]{2,1,0:T(8,128)(2,1)S(1)}, bf16[4,512,768]{2,1,0:T(8,128)(2,1)}, u32[]{:S(2)}) copy-start(bf16[4,512,768]{2,1,0:T(8,128)(2,1)} %param.9) | copy-start | bytes 9437188
  16.8 4.5 %copy-start.4 = (bf16[768,768]{1,0:T(8,128)(2,1)S(1)}, bf16[768,768]{1,0:T(8,128)(2,1)}, u32[]{:S(2)}) copy-start(bf16[768,768]{1,0:T(8,128)(2,1)} %param.13) | copy-start | bytes 3538948
  31.3 4.8 %copy-start.2 = (bf16[4,512,768]{1,2,0:T(8,128)(2,1)S(1)}, bf16[4,512,768]{1,2,0:T(8,128)(2,1)}, u32[]{:S(2)}) copy-start(bf16[4,512,768]{1,2,0:T(8,128)(2,1)} %copy.43) | copy-start | bytes 9437188
  40.2 49.2 %copy-start.5 = (s32[4]{0:T(128)S(1)}, s32[4]{0:T(128)}, u32[]{:S(2)}) copy-start(s32[4]{0:T(128)} %param.17) | copy-start | bytes 52
Sparse Core Ops, SparseCore 0:
  40.3 63.3 all-gather.2
